TPU v7x, 256 devices: a whole 4x4x8 slice. The times are simulated.
256 devices in a mesh: slab: 4 (over x), row: 64 (over y, z, core).
Axes of the slice: x: 4, y: 4, z: 8, core: 2. Of those that a mesh axis runs over, the one named last changes fastest.
Arguments:
- forcing: bfloat16 [4, 32768, 64], P('slab', 'row'), may hold values from -6 to 6
- inflow: bfloat16 [32768, 64], P('row'), may hold values from -6 to 6
- self_solve: bfloat16 [4, 64, 512, 512], P('slab', 'row'), may hold values from -0.25 to 0.25
- greens: bfloat16 [4, 64, 20, 512, 512], P('slab', 'row'), may hold values from -0.078125 to 0.078125
- kept_cols: int32 [4, 64, 20], P('slab', 'row'), may hold values from 0 to 63, as said below
- counts: int32 [4, 64], P('slab', 'row'), may hold values from 6 to 20, as said below
Outputs:
- traces: bfloat16 [4, 32768, 64], P('slab', 'row')
Inputs may be any that keep to these rules, and one draw needn't show every extreme that they name: `kept_cols`: for each slab and tile row the 20 entries name distinct column tiles. `counts`: in every slab some tile row uses all 20 slots.
All inputs are finite; a program needn't handle non-finite values.
Results may differ from a plain program's by a relative error of at most 0.012.
Values may be sent and summed in bfloat16 or wider, within the bound.
A program may use at most 64 MiB of HBM per device.

v0:
```python
import jax
import jax.numpy as jnp
from jax import lax
from jax.sharding import PartitionSpec as P

TILE = 512


def shifted(array, axis, by):
    size = lax.axis_size(axis)
    pairs = [(i, i + by) for i in range(size) if 0 <= i + by < size]
    return lax.ppermute(array, axis, pairs)


def advance(previous, inflow_cols, forcing_cols, green_row, cols_row, count_row, solve_row):
    arrived = shifted(previous, "slab", 1)
    first_slab = lax.axis_index("slab") == 0
    incoming = jnp.where(first_slab, inflow_cols, arrived)
    gathered = lax.all_gather(incoming, "row", axis=0, tiled=True)
    width = incoming.shape[1]
    tiles = gathered.reshape(-1, TILE, width)
    chosen = tiles[cols_row]
    slot_ids = jnp.arange(green_row.shape[0], dtype=jnp.int32)
    valid = slot_ids < count_row
    chosen = jnp.where(valid[:, None, None], chosen, jnp.zeros((), chosen.dtype))
    total = jnp.einsum("kij,kjw->iw", green_row, chosen, preferred_element_type=jnp.float32)
    coupled = (total + forcing_cols.astype(jnp.float32)).astype(jnp.bfloat16)
    return jnp.dot(solve_row, coupled, preferred_element_type=jnp.float32).astype(jnp.bfloat16)


def shards(forcing, inflow, self_solve, greens, kept_cols, counts):
    slab_count = lax.axis_size("slab")
    green_row = greens[0, 0]
    cols_row = kept_cols[0, 0]
    count_row = counts[0, 0]
    solve_row = self_solve[0, 0]
    source = forcing[0]
    columns = source.shape[1]
    previous = jnp.zeros((TILE, columns), jnp.bfloat16)
    for section in range(slab_count):
        previous = advance(previous, inflow, source, green_row, cols_row, count_row, solve_row)
    return previous[None]


def solution(mesh):
    placed = (
        P("slab", "row", None),
        P("row", None),
        P("slab", "row", None, None),
        P("slab", "row", None, None, None),
        P("slab", "row", None),
        P("slab", "row"),
    )
    return jax.shard_map(
        shards, mesh=mesh, in_specs=placed, out_specs=P("slab", "row", None), check_vma=False
    )
```

profile of v0, /device:TPU:1, one launch (start us, length us, event | category | flops | bytes accessed | tf_op | source)
XLA Modules:
  0.0 408.7 jit_solution(2446877907097513772)
XLA Ops:
  6.5 4.1 collective-permute-start
  11.9 1.5 broadcast_select_fusion.3
  14.8 79.0 %all-gather.5.cloned.1.call-done = bf16[32768,64]{0,1:T(8,128)(2,1)} async-done(((bf16[512,64]{0,1:T(8,128)(2,1)}), bf16[32768,64]{0,1:T(8,128)(2,1)}) %all-gather.5.cloned.1.call-update) | async-done | bytes 4194320 | tf_op jit(solution)/shard_map/all_gather | solution.py:19
  93.8 4.8 %copy.22 = bf16[8,64,8,512]{3,2,0,1:T(8,128)(2,1)} copy(bf16[8,64,8,512]{3,2,1,0:T(8,128)(2,1)} %bitcast.176) | data formatting | bytes 8388608 | tf_op jit(solution)/shard_map/reshape | solution.py:21
  98.6 2.8 gather_fusion
  101.5 7.5 %fusion.131 = bf16[512,64]{0,1:T(8,128)(2,1)S(1)} fusion(bf16[1,1,20,512,512]{4,3,2,1,0:T(8,128)(2,1)} %param.9, bf16[20,512,64]{1,2,0:T(8,128)(2,1)S(1)} %gather_fusion, pred[20]{0:T(512)(128)(4,1)S(1)} %iota_compare_fusion, bf16[1,1,512,512]{3,2,1,0:T(8,128)(2,1)S(1)} %copy-done, bf16[1,512,64]{1,2,0:T(8,128)(2,1)S(1)} %copy-done.1), kind=kOutput, calls=%fused_computation.47 | convolution fusion | flops 705429504 | bytes 12451860 | tf_op jit(solution)/shard_map/dot_general | solution.py:28
  109.0 3.1 collective-permute-start.1
  112.1 1.3 collective-permute-done.1
  114.2 77.3 %all-gather.7.cloned.1.call-done = bf16[32768,64]{0,1:T(8,128)(2,1)} async-done(((bf16[512,64]{0,1:T(8,128)(2,1)}), bf16[32768,64]{0,1:T(8,128)(2,1)}) %all-gather.7.cloned.1.call-update) | async-done | bytes 4194320 | tf_op jit(solution)/shard_map/all_gather | solution.py:19
  191.4 4.8 %copy.21 = bf16[8,64,8,512]{3,2,0,1:T(8,128)(2,1)} copy(bf16[8,64,8,512]{3,2,1,0:T(8,128)(2,1)} %bitcast.177) | data formatting | bytes 8388608 | tf_op jit(solution)/shard_map/reshape | solution.py:21
  196.2 2.8 gather_fusion.1
  199.1 7.4 %fusion.126 = bf16[512,64]{0,1:T(8,128)(2,1)S(1)} fusion(bf16[1,1,20,512,512]{4,3,2,1,0:T(8,128)(2,1)} %param.9, bf16[20,512,64]{1,2,0:T(8,128)(2,1)S(1)} %gather_fusion.1, pred[20]{0:T(512)(128)(4,1)S(1)} %iota_compare_fusion, bf16[1,1,512,512]{3,2,1,0:T(8,128)(2,1)S(1)} %copy-done, bf16[1,512,64]{1,2,0:T(8,128)(2,1)S(1)} %copy-done.1), kind=kOutput, calls=%fused_computation.46 | convolution fusion | flops 705429504 | bytes 12451860 | tf_op jit(solution)/shard_map/dot_general | solution.py:28
  206.5 3.1 collective-permute-start.2
  209.6 1.3 collective-permute-done.2
  211.6 77.3 %all-gather.9.cloned.1.call-done = bf16[32768,64]{0,1:T(8,128)(2,1)} async-done(((bf16[512,64]{0,1:T(8,128)(2,1)}), bf16[32768,64]{0,1:T(8,128)(2,1)}) %all-gather.9.cloned.1.call-update) | async-done | bytes 4194320 | tf_op jit(solution)/shard_map/all_gather | solution.py:19
  288.9 4.8 %copy.20 = bf16[8,64,8,512]{3,2,0,1:T(8,128)(2,1)} copy(bf16[8,64,8,512]{3,2,1,0:T(8,128)(2,1)} %bitcast.178) | data formatting | bytes 8388608 | tf_op jit(solution)/shard_map/reshape | solution.py:21
  293.7 2.8 gather_fusion.2
  296.6 7.4 %fusion.121 = bf16[512,64]{0,1:T(8,128)(2,1)S(1)} fusion(bf16[1,1,20,512,512]{4,3,2,1,0:T(8,128)(2,1)} %param.9, bf16[20,512,64]{1,2,0:T(8,128)(2,1)S(1)} %gather_fusion.2, pred[20]{0:T(512)(128)(4,1)S(1)} %iota_compare_fusion, bf16[1,1,512,512]{3,2,1,0:T(8,128)(2,1)S(1)} %copy-done, bf16[1,512,64]{1,2,0:T(8,128)(2,1)S(1)} %copy-done.1), kind=kOutput, calls=%fused_computation.45 | convolution fusion | flops 705429504 | bytes 12451860 | tf_op jit(solution)/shard_map/dot_general | solution.py:28
  304.0 3.1 collective-permute-start.3
  307.1 1.3 collective-permute-done.3
  309.1 77.3 %all-gather.11.cloned.1.call-done = bf16[32768,64]{0,1:T(8,128)(2,1)} async-done(((bf16[512,64]{0,1:T(8,128)(2,1)}), bf16[32768,64]{0,1:T(8,128)(2,1)}) %all-gather.11.cloned.1.call-update) | async-done | bytes 4194320 | tf_op jit(solution)/shard_map/all_gather | solution.py:19
  386.4 4.8 %copy.19 = bf16[8,64,8,512]{3,2,0,1:T(8,128)(2,1)} copy(bf16[8,64,8,512]{3,2,1,0:T(8,128)(2,1)} %bitcast.179) | data formatting | bytes 8388608 | tf_op jit(solution)/shard_map/reshape | solution.py:21
  391.2 2.8 gather_fusion.3
  394.1 8.1 %fusion.116 = bf16[1,512,64]{1,2,0:T(8,128)(2,1)} fusion(bf16[1,1,20,512,512]{4,3,2,1,0:T(8,128)(2,1)} %param.9, bf16[20,512,64]{1,2,0:T(8,128)(2,1)S(1)} %gather_fusion.3, pred[20]{0:T(512)(128)(4,1)S(1)} %iota_compare_fusion, bf16[1,1,512,512]{3,2,1,0:T(8,128)(2,1)S(1)} %copy-done, bf16[1,512,64]{1,2,0:T(8,128)(2,1)S(1)} %copy-done.1), kind=kOutput, calls=%fused_computation.44 | convolution fusion | flops 705429504 | bytes 12451860 | tf_op jit(solution)/shard_map/dot_general | solution.py:28
  (22 shorter events, 4.1 us)
Async XLA Ops:
  6.5 95.0 %copy-start = (bf16[1,1,512,512]{3,2,1,0:T(8,128)(2,1)S(1)}, bf16[1,1,512,512]{3,2,1,0:T(8,128)(2,1)}, u32[]{:S(2)}) copy-start(bf16[1,1,512,512]{3,2,1,0:T(8,128)(2,1)} %param.8) | copy-start | bytes 1572868
  6.5 87.3 %all-gather.5.cloned.1.call-start = ((), (), s32[]{:S(2)}) async-start(), calls=%async_computation | async-start | bytes 4259840 | tf_op jit(solution)/shard_map/all_gather | solution.py:19
  6.5 5.4 %collective-permute-start = (bf16[512,64]{0,1:T(8,128)(2,1)S(1)}, bf16[512,64]{0,1:T(8,128)(2,1)S(1)}, u32[]{:S(2)}, u32[]{:S(2)}) collective-permute-start(bf16[512,64]{0,1:T(8,128)(2,1)S(1)} %broadcast_in_dim.39), channel_id=1, source_target_pairs={{0,64},{64,128},{128,192},{1,65},{65,129},{129,193},{2,66},{66,130... | collective-permute-start | bytes 196616 | tf_op jit(solution)/shard_map/ppermute | solution.py:12
  13.4 178.0 %all-gather.7.cloned.1.call-start = ((), (), s32[]{:S(2)}) async-start(), calls=%async_computation.1 | async-start | bytes 4259840 | tf_op jit(solution)/shard_map/all_gather | solution.py:19
  98.6 2.9 copy-start.1
  101.5 11.9 %copy-start.2 = (bf16[512,64]{0,1:T(8,128)(2,1)S(1)}, bf16[512,64]{0,1:T(8,128)(2,1)}, u32[]{:S(2)}) copy-start(bf16[512,64]{0,1:T(8,128)(2,1)} %param.7) | copy-start | bytes 196612
  109.0 4.4 %collective-permute-start.1 = (bf16[512,64]{0,1:T(8,128)(2,1)S(1)}, bf16[512,64]{0,1:T(8,128)(2,1)S(1)}, u32[]{:S(2)}, u32[]{:S(2)}) collective-permute-start(bf16[512,64]{0,1:T(8,128)(2,1)S(1)} %fusion.131), channel_id=1, source_target_pairs={{0,64},{64,128},{128,192},{1,65},{65,129},{129,193},{2,66},{66,130... | collective-permute-start | bytes 196616 | tf_op jit(solution)/shard_map/ppermute | solution.py:12
  114.1 174.8 %all-gather.9.cloned.1.call-start = ((), (), s32[]{:S(2)}) async-start(), calls=%async_computation.2 | async-start | bytes 4259840 | tf_op jit(solution)/shard_map/all_gather | solution.py:19
  206.5 4.4 %collective-permute-start.2 = (bf16[512,64]{0,1:T(8,128)(2,1)S(1)}, bf16[512,64]{0,1:T(8,128)(2,1)S(1)}, u32[]{:S(2)}, u32[]{:S(2)}) collective-permute-start(bf16[512,64]{0,1:T(8,128)(2,1)S(1)} %fusion.126), channel_id=1, source_target_pairs={{0,64},{64,128},{128,192},{1,65},{65,129},{129,193},{2,66},{66,130... | collective-permute-start | bytes 196616 | tf_op jit(solution)/shard_map/ppermute | solution.py:12
  211.6 174.8 %all-gather.11.cloned.1.call-start = ((), (), s32[]{:S(2)}) async-start(), calls=%async_computation.3 | async-start | bytes 4259840 | tf_op jit(solution)/shard_map/all_gather | solution.py:19
  304.0 4.4 %collective-permute-start.3 = (bf16[512,64]{0,1:T(8,128)(2,1)S(1)}, bf16[512,64]{0,1:T(8,128)(2,1)S(1)}, u32[]{:S(2)}, u32[]{:S(2)}) collective-permute-start(bf16[512,64]{0,1:T(8,128)(2,1)S(1)} %fusion.121), channel_id=1, source_target_pairs={{0,64},{64,128},{128,192},{1,65},{65,129},{129,193},{2,66},{66,130... | collective-permute-start | bytes 196616 | tf_op jit(solution)/shard_map/ppermute | solution.py:12
Sparse Core Ops, SparseCore 0:
  13.6 80.2 all-gather.4
  114.2 77.1 all-gather.6
  211.7 77.1 all-gather.8
  309.2 77.1 all-gather.10
where the time goes:
time: 409 us
  waiting for transfers between devices  316 us (77%)
  local copies, waits for them, and re-layouts  30.5 us (7%)
  matrix products  30.5 us (7%)
  between operations  13.9 us (3%)
  starting transfers between devices  13.5 us (3%)
    all_gather x4, waiting for transfers between devices, advance(): gathered = lax.all_gather(incoming, 'row', axis=0, tiled=True)  311 us
    dot_general x4, matrix products, advance(): jnp.dot(solve_row, coupled, preferred_element_type=jnp.float32)  30.5 us
    reshape x4, local copies, waits for them, and re-layouts, advance(): tiles = gathered.reshape(-1, TILE, width)  19.2 us
    ppermute x4, starting transfers between devices, shifted(): return lax.ppermute(array, axis, pairs)  13.4 us
    gather x4, local copies, waits for them, and re-layouts, advance(): chosen = tiles[cols_row]  11.3 us
  transfers between devices with their start and end apart: 8, of which 8 were waited for; matrix products, arithmetic and copies ran while one was open for 0% of the time, Pallas kernels for 0%

commit v1 on v0

--- a/solution.py
+++ b/solution.py
@@ -16,7 +16,9 @@
     arrived = shifted(previous, "slab", 1)
     first_slab = lax.axis_index("slab") == 0
     incoming = jnp.where(first_slab, inflow_cols, arrived)
-    gathered = lax.all_gather(incoming, "row", axis=0, tiled=True)
+    gathered = jnp.concatenate(
+        lax.all_to_all(jnp.stack([incoming] * lax.axis_size("row")), "row", 0, 0), axis=0
+    )
     width = incoming.shape[1]
     tiles = gathered.reshape(-1, TILE, width)
     chosen = tiles[cols_row]

time: 409 us -> 485 us (1.19)
  blocking collectives: 0 us -> 308 us
  waiting for transfers between devices: 316 us -> 100 us
  local copies, waits for them, and re-layouts: 30.5 us -> 15.3 us
  starting transfers between devices: 13.5 us -> 28.7 us
  between operations: 13.9 us -> 0.85 us
    all_gather x4 -> x0, waiting for transfers between devices: 311 us -> none  [advance(): gathered = lax.all_gather(incoming, 'row', axis=0, tiled=True)]
    all_to_all x0 -> x3, blocking collectives: none -> 308 us  [advance(): lax.all_to_all(jnp.stack([incoming] * lax.axis_size('row')), 'row', 0, 0)]
    all_to_all x0 -> x1, waiting for transfers between devices: none -> 95.1 us  [advance(): lax.all_to_all(jnp.stack([incoming] * lax.axis_size('row')), 'row', 0, 0)]
    reshape x4 -> x0, local copies, waits for them, and re-layouts: 19.2 us -> none  [advance(): tiles = gathered.reshape(-1, TILE, width)]
    all_to_all x0 -> x1, starting transfers between devices: none -> 13.5 us  [advance(): lax.all_to_all(jnp.stack([incoming] * lax.axis_size('row')), 'row', 0, 0)]
  transfers between devices with their start and end apart: 8 -> 5, of which waited for: 8 -> 5; matrix products, arithmetic and copies ran while one was open for 0% -> 0% of each run, Pallas kernels for 0% -> 0%
where the time goes in v1:
time: 485 us; the launch traced here: 484 us
  blocking collectives  308 us (64%)
  waiting for transfers between devices  100 us (21%)
  matrix products  30.5 us (6%)
  starting transfers between devices  28.7 us (6%)
  local copies, waits for them, and re-layouts  15.3 us (3%)
    all_to_all x3, blocking collectives, advance(): lax.all_to_all(jnp.stack([incoming] * lax.axis_size('row')), 'row', 0, 0)  308 us
    all_to_all x1, waiting for transfers between devices, advance(): lax.all_to_all(jnp.stack([incoming] * lax.axis_size('row')), 'row', 0, 0)  95.1 us
    dot_general x4, matrix products, advance(): jnp.dot(solve_row, coupled, preferred_element_type=jnp.float32)  30.5 us
    ppermute x4, starting transfers between devices, shifted(): return lax.ppermute(array, axis, pairs)  15.2 us
    all_to_all x1, starting transfers between devices, advance(): lax.all_to_all(jnp.stack([incoming] * lax.axis_size('row')), 'row', 0, 0)  13.5 us
    gather x4, local copies, waits for them, and re-layouts, advance(): chosen = tiles[cols_row]  11.3 us
  transfers between devices with their start and end apart: 5, of which 5 were waited for; matrix products, arithmetic and copies ran while one was open for 0% of the time, Pallas kernels for 0%

profile of v1, /device:TPU:1, one launch (start us, length us, event | category | flops | bytes accessed | tf_op | source)
XLA Modules:
  0.0 484.4 jit_solution(18372437495070279112)
XLA Ops:
  0.0 4.1 collective-permute-start
  4.1 1.3 collective-permute-done
  5.4 0.8 broadcast_select_fusion.3
  6.2 2.5 stack.8
  8.7 13.5 %all-to-all-start = ((bf16[64,512,64]{1,2,0:T(8,128)(2,1)}), bf16[64,512,64]{1,2,0:T(8,128)(2,1)}, u32[]{:S(2)}, u32[]{:S(2)}) async-start(bf16[64,512,64]{1,2,0:T(8,128)(2,1)} %stack.8), calls=%async_computation | async-start | bytes 8388608 | tf_op jit(solution)/shard_map/all_to_all | solution.py:20
  22.9 95.1 %all-to-all-done = bf16[64,512,64]{1,2,0:T(8,128)(2,1)} async-done(((bf16[64,512,64]{1,2,0:T(8,128)(2,1)}), bf16[64,512,64]{1,2,0:T(8,128)(2,1)}, u32[]{:S(2)}, u32[]{:S(2)}) %all-to-all-start) | async-done | bytes 4194336 | tf_op jit(solution)/shard_map/all_to_all | solution.py:20
  118.1 2.8 gather_fusion
  121.0 7.5 %fusion.131 = bf16[512,64]{0,1:T(8,128)(2,1)S(1)} fusion(bf16[1,1,20,512,512]{4,3,2,1,0:T(8,128)(2,1)} %param.9, bf16[20,512,64]{1,2,0:T(8,128)(2,1)S(1)} %gather_fusion, pred[20]{0:T(512)(128)(4,1)S(1)} %iota_compare_fusion, bf16[1,1,512,512]{3,2,1,0:T(8,128)(2,1)S(1)} %copy-done, bf16[1,512,64]{1,2,0:T(8,128)(2,1)S(1)} %copy-done.1), kind=kOutput, calls=%fused_computation.43 | convolution fusion | flops 705429504 | bytes 12451860 | tf_op jit(solution)/shard_map/dot_general | solution.py:30
  128.4 3.2 collective-permute-start.1
  131.6 1.3 collective-permute-done.1
  132.9 0.5 stack.9
  133.4 102.4 %all_to_all.20 = bf16[64,512,64]{1,2,0:T(8,128)(2,1)} all-to-all(bf16[64,512,64]{1,2,0:T(8,128)(2,1)S(1)} %stack.9), channel_id=1, replica_groups=mesh['slab'=4,'row'=64] {'row'}, dimensions={0} | all-to-all | bytes 8388608 | tf_op jit(solution)/shard_map/all_to_all | solution.py:20
  235.9 2.8 gather_fusion.1
  238.7 7.4 %fusion.126 = bf16[512,64]{0,1:T(8,128)(2,1)S(1)} fusion(bf16[1,1,20,512,512]{4,3,2,1,0:T(8,128)(2,1)} %param.9, bf16[20,512,64]{1,2,0:T(8,128)(2,1)S(1)} %gather_fusion.1, pred[20]{0:T(512)(128)(4,1)S(1)} %iota_compare_fusion, bf16[1,1,512,512]{3,2,1,0:T(8,128)(2,1)S(1)} %copy-done, bf16[1,512,64]{1,2,0:T(8,128)(2,1)S(1)} %copy-done.1), kind=kOutput, calls=%fused_computation.42 | convolution fusion | flops 705429504 | bytes 12451860 | tf_op jit(solution)/shard_map/dot_general | solution.py:30
  246.1 4.0 collective-permute-start.2
  250.1 1.3 collective-permute-done.2
  252.0 102.7 %all_to_all.21 = bf16[64,512,64]{1,2,0:T(8,128)(2,1)} all-to-all(bf16[64,512,64]{1,2,0:T(8,128)(2,1)S(1)} %stack.10), channel_id=1, replica_groups=mesh['slab'=4,'row'=64] {'row'}, dimensions={0} | all-to-all | bytes 8388608 | tf_op jit(solution)/shard_map/all_to_all | solution.py:20
  354.7 2.8 gather_fusion.2
  357.5 7.4 %fusion.121 = bf16[512,64]{0,1:T(8,128)(2,1)S(1)} fusion(bf16[1,1,20,512,512]{4,3,2,1,0:T(8,128)(2,1)} %param.9, bf16[20,512,64]{1,2,0:T(8,128)(2,1)S(1)} %gather_fusion.2, pred[20]{0:T(512)(128)(4,1)S(1)} %iota_compare_fusion, bf16[1,1,512,512]{3,2,1,0:T(8,128)(2,1)S(1)} %copy-done, bf16[1,512,64]{1,2,0:T(8,128)(2,1)S(1)} %copy-done.1), kind=kOutput, calls=%fused_computation.41 | convolution fusion | flops 705429504 | bytes 12451860 | tf_op jit(solution)/shard_map/dot_general | solution.py:30
  365.0 4.0 collective-permute-start.3
  369.0 1.3 collective-permute-done.3
  370.8 102.7 %all_to_all.22 = bf16[64,512,64]{1,2,0:T(8,128)(2,1)} all-to-all(bf16[64,512,64]{1,2,0:T(8,128)(2,1)S(1)} %stack.11), channel_id=1, replica_groups=mesh['slab'=4,'row'=64] {'row'}, dimensions={0} | all-to-all | bytes 8388608 | tf_op jit(solution)/shard_map/all_to_all | solution.py:20
  473.5 2.8 gather_fusion.3
  476.4 8.1 %fusion.116 = bf16[1,512,64]{1,2,0:T(8,128)(2,1)} fusion(bf16[1,1,20,512,512]{4,3,2,1,0:T(8,128)(2,1)} %param.9, bf16[20,512,64]{1,2,0:T(8,128)(2,1)S(1)} %gather_fusion.3, pred[20]{0:T(512)(128)(4,1)S(1)} %iota_compare_fusion, bf16[1,1,512,512]{3,2,1,0:T(8,128)(2,1)S(1)} %copy-done, bf16[1,512,64]{1,2,0:T(8,128)(2,1)S(1)} %copy-done.1), kind=kOutput, calls=%fused_computation.40 | convolution fusion | flops 705429504 | bytes 12451860 | tf_op jit(solution)/shard_map/dot_general | solution.py:30
  (17 shorter events, 1.1 us)
Async XLA Ops:
  0.0 120.9 %copy-start = (bf16[1,1,512,512]{3,2,1,0:T(8,128)(2,1)S(1)}, bf16[1,1,512,512]{3,2,1,0:T(8,128)(2,1)}, u32[]{:S(2)}) copy-start(bf16[1,1,512,512]{3,2,1,0:T(8,128)(2,1)} %param.8) | copy-start | bytes 1572868
  0.0 5.4 %collective-permute-start = (bf16[512,64]{0,1:T(8,128)(2,1)S(1)}, bf16[512,64]{0,1:T(8,128)(2,1)S(1)}, u32[]{:S(2)}, u32[]{:S(2)}) collective-permute-start(bf16[512,64]{0,1:T(8,128)(2,1)S(1)} %broadcast_in_dim.39), channel_id=1, source_target_pairs={{0,64},{64,128},{128,192},{1,65},{65,129},{129,193},{2,66},{66,130... | collective-permute-start | bytes 196616 | tf_op jit(solution)/shard_map/ppermute | solution.py:12
  8.7 14.2 %copy-start.3 = (s32[1,1,20]{2,1,0:T(1,128)S(1)}, s32[1,1,20]{2,1,0:T(1,128)}, u32[]{:S(2)}) copy-start(s32[1,1,20]{2,1,0:T(1,128)} %param.10) | copy-start | bytes 244
  8.7 109.4 %all-to-all-start = ((bf16[64,512,64]{1,2,0:T(8,128)(2,1)}), bf16[64,512,64]{1,2,0:T(8,128)(2,1)}, u32[]{:S(2)}, u32[]{:S(2)}) async-start(bf16[64,512,64]{1,2,0:T(8,128)(2,1)} %stack.8), calls=%async_computation | async-start | bytes 8388608 | tf_op jit(solution)/shard_map/all_to_all | solution.py:20
  22.9 98.0 %copy-start.1 = (bf16[1,512,64]{1,2,0:T(8,128)(2,1)S(1)}, bf16[1,512,64]{1,2,0:T(8,128)(2,1)}, u32[]{:S(2)}) copy-start(bf16[1,512,64]{1,2,0:T(8,128)(2,1)} %param.6) | copy-start | bytes 196612
  120.9 12.0 %copy-start.2 = (bf16[512,64]{0,1:T(8,128)(2,1)S(1)}, bf16[512,64]{0,1:T(8,128)(2,1)}, u32[]{:S(2)}) copy-start(bf16[512,64]{0,1:T(8,128)(2,1)} %param.7) | copy-start | bytes 196612
  128.4 4.5 collective-permute-start.1
  246.1 5.3 %collective-permute-start.2 = (bf16[512,64]{0,1:T(8,128)(2,1)S(1)}, bf16[512,64]{0,1:T(8,128)(2,1)S(1)}, u32[]{:S(2)}, u32[]{:S(2)}) collective-permute-start(bf16[512,64]{0,1:T(8,128)(2,1)S(1)} %fusion.126), channel_id=1, source_target_pairs={{0,64},{64,128},{128,192},{1,65},{65,129},{129,193},{2,66},{66,130... | collective-permute-start | bytes 196616 | tf_op jit(solution)/shard_map/ppermute | solution.py:12
  365.0 5.3 %collective-permute-start.3 = (bf16[512,64]{0,1:T(8,128)(2,1)S(1)}, bf16[512,64]{0,1:T(8,128)(2,1)S(1)}, u32[]{:S(2)}, u32[]{:S(2)}) collective-permute-start(bf16[512,64]{0,1:T(8,128)(2,1)S(1)} %fusion.121), channel_id=1, source_target_pairs={{0,64},{64,128},{128,192},{1,65},{65,129},{129,193},{2,66},{66,130... | collective-permute-start | bytes 196616 | tf_op jit(solution)/shard_map/ppermute | solution.py:12
